TPU v7x, 32 devices: a whole 2x2x4 slice. The times are simulated.
32 devices in a mesh: pix: 4 (over y, core), chan: 8 (over z, x).
Axes of the slice: x: 2, y: 2, z: 4, core: 2. Of those that a mesh axis runs over, the one named last changes fastest.
Arguments:
- images: bfloat16 [2048, 32, 128], P('pix', 'chan'), may hold values from -6 to 6
- conv_weight: float32 [2048, 49], P('pix'), may hold values from -6 to 6
- conv_bias: float32 [2048], P('pix'), may hold values from -4 to 4
- norm_gain: float32 [2048], replicated, may hold values from 0.25 to 1.75
- norm_shift: float32 [2048], replicated, may hold values from -3 to 3
- up_weight: bfloat16 [2048, 8192], P(None, 'pix'), may hold values from -0.125 to 0.125
- up_bias: float32 [8192], P('pix'), may hold values from -3 to 3
- down_weight: bfloat16 [2048, 8192], P(None, 'pix'), may hold values from -0.09375 to 0.09375
- down_bias: float32 [2048], P('pix'), may hold values from -3 to 3
- layer_scale: float32 [2048], P('pix'), may hold values from 0.5 to 2
Outputs:
- block_out: bfloat16 [2048, 32, 128], P('pix', 'chan')
All inputs are finite; a program needn't handle non-finite values.
Results may differ from a plain program's by a relative error of at most 0.006.
Values may be sent and summed in bfloat16 or wider, within the bound.
A program may use at most 64 MiB of HBM per device.

v0:
```python
import jax
import jax.numpy as jnp
from jax import lax
from jax.sharding import PartitionSpec as P

C = 2048


def with_halo(block, sides, width):
    for axis, dim in sides:
        count = lax.axis_size(axis)
        forward = [(i, i + 1) for i in range(count - 1)]
        backward = [(target, source) for source, target in forward]
        low = lax.ppermute(
            lax.slice_in_dim(block, block.shape[dim] - width, None, axis=dim), axis, forward
        )
        high = lax.ppermute(lax.slice_in_dim(block, 0, width, axis=dim), axis, backward)
        block = jnp.concatenate([low, block, high], axis=dim)
    return block


def on_device(
    images,
    conv_weight,
    conv_bias,
    norm_gain,
    norm_shift,
    up_weight,
    up_bias,
    down_weight,
    down_bias,
    layer_scale,
):
    chans, rows, width = images.shape
    pixels = rows * width
    padded = with_halo(images, (("chan", 1),), 3)
    wide = jnp.pad(padded.astype(jnp.float32), ((0, 0), (0, 0), (3, 3)))
    total = jnp.zeros((chans, rows, width), jnp.float32)
    for first in range(7):
        for second in range(7):
            total = (
                total
                + conv_weight[:, first * 7 + second][:, None, None]
                * wide[:, first : first + rows, second : second + width]
            )
    filtered = (total + conv_bias[:, None, None]).astype(jnp.bfloat16).reshape(chans, pixels)
    values = filtered.astype(jnp.float32)
    sum_first, sum_second = lax.psum(
        (jnp.sum(values, axis=0), jnp.sum(values * values, axis=0)), "pix"
    )
    mean = sum_first / C
    var = sum_second / C - mean * mean
    offset = lax.axis_index("pix") * chans
    gain_local = lax.dynamic_slice_in_dim(norm_gain, offset, chans, 0)
    shift_local = lax.dynamic_slice_in_dim(norm_shift, offset, chans, 0)
    normed_local = (
        (values - mean) * lax.rsqrt(var + 1e-06) * gain_local[:, None] + shift_local[:, None]
    ).astype(jnp.bfloat16)
    gathered = lax.all_gather(normed_local, "pix", axis=0, tiled=True)
    contract = (((0,), (0,)), ((), ()))
    pre = lax.dot_general(up_weight, gathered, contract, preferred_element_type=jnp.float32)
    hidden = jax.nn.gelu(pre + up_bias[:, None], approximate=True).astype(jnp.bfloat16)
    terms = jnp.dot(down_weight, hidden, preferred_element_type=jnp.float32)
    mixed = lax.psum_scatter(terms, "pix", scatter_dimension=0, tiled=True)
    result = images.astype(jnp.float32).reshape(chans, pixels) + layer_scale[:, None] * (
        mixed + down_bias[:, None]
    )
    return result.astype(jnp.bfloat16).reshape(chans, rows, width)


def solution(mesh):
    placed = (
        P("pix", "chan", None),
        P("pix", None),
        P("pix"),
        P(),
        P(),
        P(None, "pix"),
        P("pix"),
        P(None, "pix"),
        P("pix"),
        P("pix"),
    )
    return jax.shard_map(
        on_device, mesh=mesh, in_specs=placed, out_specs=P("pix", "chan", None), check_vma=False
    )
```

profile of v0, /device:TPU:0, one launch (start us, length us, event | category | flops | bytes accessed | tf_op | source)
XLA Modules:
  0.0 194.6 jit_solution(2396810698593595446)
XLA Ops:
  6.5 0.0 copy-start.3
  6.5 0.0 all-gather.2.cloned.1.call-start
  6.5 1.7 fusion.103
  8.2 4.9 %collective-permute-start = (bf16[512,3,128]{2,1,0:T(4,128)(2,1)S(1)}, bf16[512,3,128]{2,1,0:T(4,128)(2,1)S(1)}, u32[]{:S(2)}, u32[]{:S(2)}) collective-permute-start(bf16[512,3,128]{2,1,0:T(4,128)(2,1)S(1)} %get-tuple-element.10), channel_id=1, source_target_pairs={{0,1},{1,2},{2,3},{3,4},{4,5},{5,6},{6,7},{8,9},{9,10},{10,11},{11... | collective-permute-start | bytes 1179656 | tf_op jit(solution)/shard_map/ppermute | solution.py:14
  13.1 1.3 collective-permute-start.1
  14.5 1.1 fusion.104
  15.6 0.8 dynamic_slice.6
  16.4 0.8 dynamic_slice.7
  17.1 1.0 fusion.106
  18.1 1.2 fusion.105
  19.2 16.3 %collective-permute-done = bf16[512,3,128]{2,1,0:T(4,128)(2,1)S(1)} collective-permute-done((bf16[512,3,128]{2,1,0:T(4,128)(2,1)S(1)}, bf16[512,3,128]{2,1,0:T(4,128)(2,1)S(1)}, u32[]{:S(2)}, u32[]{:S(2)}) %collective-permute-start) | collective-permute-done | bytes 393248 | tf_op jit(solution)/shard_map/ppermute | solution.py:14
  35.5 0.0 collective-permute-done.1
  35.5 2.2 %maximum_convert_fusion = f32[512,10,128]{2,1,0:T(8,128)S(1)} fusion(bf16[512,3,128]{2,1,0:T(4,128)(2,1)S(1)} %collective-permute-done.1, bf16[512,4,128]{2,1,0:T(4,128)(2,1)} %param.10, bf16[512,3,128]{2,1,0:T(4,128)(2,1)S(1)} %collective-permute-done), kind=kLoop, calls=%fused_computation.52 | loop fusion | flops 3932160 | bytes 3932160 | tf_op jit(solution)/shard_map/convert_element_type | solution.py:37
  37.7 0.0 copy-done.3
  37.7 0.0 copy-start.4
  37.7 52.7 %convert_reduce_fusion = (f32[4,128]{1,0:T(4,128)S(1)}, f32[4,128]{1,0:T(4,128)S(1)}, bf16[512,4,128]{2,1,0:T(4,128)(2,1)S(1)}) fusion(f32[512]{0:T(512)S(1)} %copy-done.3, f32[512]{0:T(512)S(1)} %bitcast.118, f32[512]{0:T(512)S(1)} %bitcast.119, f32[512]{0:T(512)S(1)} %bitcast.91, f32[512,10,128]{2,1,0:T(8,128)S(1)} %maximum_convert_fusion, ...), kind=kLoop, calls=%fused_computation.159 | loop fusion | flops 26999808 | bytes 12165120 | tf_op jit(solution)/shard_map/reduce_sum | solution.py:49
  90.4 0.1 convert.2
  90.6 5.8 %all-reduce.1 = (f32[512]{0:T(512)S(1)}, f32[512]{0:T(512)S(1)}) all-reduce(f32[512]{0:T(512)S(1)} %bitcast.140, f32[512]{0:T(512)S(1)} %bitcast.139), channel_id=1, replica_groups=mesh['pix'=4,'chan'=8] {'pix'}, use_global_device_ids=true, to_apply=%region_3.4 | all-reduce | flops 1024 | bytes 8192 | tf_op jit(solution)/shard_map/psum | solution.py:48
  96.3 1.0 fusion.101
  97.4 0.0 all-gather.2.cloned.1.call-update
  97.4 0.2 reduce-scatter.2.cloned.1.call-start
  97.6 24.9 %all-gather.2.cloned.1.call-done = bf16[2048,512]{1,0:T(8,128)(2,1)} async-done(((bf16[512,512]{1,0:T(8,128)(2,1)}), bf16[2048,512]{1,0:T(8,128)(2,1)}) %all-gather.2.cloned.1.call-update) | async-done | bytes 2097168 | tf_op jit(solution)/shard_map/all_gather | solution.py:59
  122.5 0.0 copy-done.4
  122.5 18.1 %convolution_bitcast_fusion = f32[2048,512]{0,1:T(8,128)} fusion(bf16[2048,2048]{1,0:T(8,128)(2,1)} %param.17, bf16[2048,512]{1,0:T(8,128)(2,1)} %all-gather.2.cloned.1.call-done, bf16[2048,2048]{1,0:T(8,128)(2,1)} %param.15, f32[2048]{0:T(1024)S(1)} %copy-done.4), kind=kOutput, calls=%fused_computation.51 | convolution fusion | flops 8600420352 | bytes 23076864 | tf_op jit(solution)/shard_map/dot_general | solution.py:63
  140.6 0.0 copy-start
  140.6 0.0 copy-start.1
  140.6 0.0 copy-start.2
  140.6 0.0 reduce-scatter.2.cloned.1.call-update
  140.6 1.0 copy-done
  141.6 0.3 copy.11
  141.9 43.2 %reduce-scatter.2.cloned.1.call-done = f32[512,512]{0,1:T(8,128)} async-done(((f32[2048,512]{0,1:T(8,128)}), f32[512,512]{0,1:T(8,128)}) %reduce-scatter.2.cloned.1.call-update) | async-done | bytes 1048592 | tf_op jit(solution)/shard_map/reduce_scatter | solution.py:64
  185.2 0.0 copy-done.1
  185.2 0.0 copy-done.2
  185.2 1.5 fusion.102
  186.6 1.1 copy.12
  (1 shorter events, 0.0 us)
Async XLA Ops:
  6.5 31.2 %copy-start.3 = (f32[512]{0:T(512)S(1)}, f32[512]{0:T(512)}, u32[]{:S(2)}) copy-start(f32[512]{0:T(512)} %param.12) | copy-start | bytes 6148
  6.5 116.0 %all-gather.2.cloned.1.call-start = ((), (), s32[]{:S(2)}) async-start(), calls=%async_computation.1 | async-start | bytes 2621440 | tf_op jit(solution)/shard_map/all_gather | solution.py:59
  8.2 27.3 %collective-permute-start = (bf16[512,3,128]{2,1,0:T(4,128)(2,1)S(1)}, bf16[512,3,128]{2,1,0:T(4,128)(2,1)S(1)}, u32[]{:S(2)}, u32[]{:S(2)}) collective-permute-start(bf16[512,3,128]{2,1,0:T(4,128)(2,1)S(1)} %get-tuple-element.10), channel_id=1, source_target_pairs={{0,1},{1,2},{2,3},{3,4},{4,5},{5,6},{6,7},{8,9},{9,10},{10,11},{11... | collective-permute-start | bytes 1179656 | tf_op jit(solution)/shard_map/ppermute | solution.py:14
  13.1 22.4 %collective-permute-start.1 = (bf16[512,3,128]{2,1,0:T(4,128)(2,1)S(1)}, bf16[512,3,128]{2,1,0:T(4,128)(2,1)S(1)}, u32[]{:S(2)}, u32[]{:S(2)}) collective-permute-start(bf16[512,3,128]{2,1,0:T(4,128)(2,1)S(1)} %get-tuple-element.11), channel_id=1, source_target_pairs={{1,0},{2,1},{3,2},{4,3},{5,4},{6,5},{7,6},{9,8},{10,9},{11,10},{12... | collective-permute-start | bytes 1179656 | tf_op jit(solution)/shard_map/ppermute | solution.py:17
  37.7 84.8 %copy-start.4 = (f32[2048]{0:T(1024)S(1)}, f32[2048]{0:T(1024)}, u32[]{:S(2)}) copy-start(f32[2048]{0:T(1024)} %param.16) | copy-start | bytes 24580
  97.4 87.8 %reduce-scatter.2.cloned.1.call-start = ((), (), s32[]{:S(2)}) async-start(), calls=%async_computation.2 | async-start | bytes 5242880 | tf_op jit(solution)/shard_map/reduce_scatter | solution.py:64
  140.6 1.0 copy-start
  140.6 44.6 %copy-start.1 = (f32[512]{0:T(512)S(1)}, f32[512]{0:T(512)}, u32[]{:S(2)}) copy-start(f32[512]{0:T(512)} %param.18) | copy-start | bytes 6148
  140.6 44.6 %copy-start.2 = (f32[512]{0:T(512)S(1)}, f32[512]{0:T(512)}, u32[]{:S(2)}) copy-start(f32[512]{0:T(512)} %param.19) | copy-start | bytes 6148
Sparse Core Ops, SparseCore 0:
  97.5 24.9 all-gather.1
  140.7 44.3 reduce-scatter.1
where the time goes:
time: 195 us
  waiting for transfers between devices  84.4 us (43%)
  other arithmetic  57.5 us (29%)
  matrix products  18.1 us (9%)
  between operations  13.5 us (7%)
  local copies, waits for them, and re-layouts  8.88 us (5%)
  starting transfers between devices  6.42 us (3%)
  blocking collectives  5.76 us (3%)
    reduce_sum x1, other arithmetic, on_device(): jnp.sum(values, axis=0)  52.7 us
    reduce_scatter x1, waiting for transfers between devices, on_device(): mixed = lax.psum_scatter(terms, 'pix', scatter_dimension=0, tiled=True)  43.2 us
    all_gather x1, waiting for transfers between devices, on_device(): gathered = lax.all_gather(normed_local, 'pix', axis=0, tiled=True)  24.9 us
    dot_general x1, matrix products, on_device(): terms = jnp.dot(down_weight, hidden, preferred_element_type=jnp.float32)  18.1 us
    ppermute x1, waiting for transfers between devices, with_halo(): lax.ppermute(lax.slice_in_dim(block, block.shape[dim] - width, None, axis...  16.3 us
    psum x1, blocking collectives, on_device(): lax.psum((jnp.sum(values, axis=0), jnp.sum(values * values, axis=0)), 'pix')  5.76 us
    ppermute x1, starting transfers between devices, with_halo(): lax.ppermute(lax.slice_in_dim(block, block.shape[dim] - width, None, axis...  4.9 us
  transfers between devices with their start and end apart: 4, of which 3 were waited for; matrix products, arithmetic and copies ran while one was open for 3% of the time, Pallas kernels for 0%

commit v1 on v0

--- a/solution.py
+++ b/solution.py
@@ -56,7 +56,14 @@
     normed_local = (
         (values - mean) * lax.rsqrt(var + 1e-06) * gain_local[:, None] + shift_local[:, None]
     ).astype(jnp.bfloat16)
-    gathered = lax.all_gather(normed_local, "pix", axis=0, tiled=True)
+    ways = lax.axis_size("pix")
+    pieces = [normed_local]
+    for far in range(1, ways):
+        pieces.append(
+            lax.ppermute(pieces[far - 1], "pix", [(d, (d - 1) % ways) for d in range(ways)])
+        )
+    line = jnp.concatenate(pieces, axis=0)
+    gathered = jnp.roll(line, lax.axis_index("pix") * normed_local.shape[0], axis=0)
     contract = (((0,), (0,)), ((), ()))
     pre = lax.dot_general(up_weight, gathered, contract, preferred_element_type=jnp.float32)
     hidden = jax.nn.gelu(pre + up_bias[:, None], approximate=True).astype(jnp.bfloat16)

time: 195 us -> 202 us (1.036)
  local copies, waits for them, and re-layouts: 8.88 us -> 14.8 us
  starting transfers between devices: 6.42 us -> 10.9 us
  waiting for transfers between devices: 84.4 us -> 80.8 us
    all_gather x1 -> x0, waiting for transfers between devices: 24.9 us -> none  [on_device(): gathered = lax.all_gather(normed_local, 'pix', axis=0, tiled=True)]
    ppermute x0 -> x3, waiting for transfers between devices: none -> 18.4 us  [on_device(): lax.ppermute(pieces[far - 1], 'pix', [(d, (d - 1) % ways) for d in range(...]
    unnamed x10 -> x16, local copies, waits for them, and re-layouts: 1.03 us -> 6.04 us
    ppermute x0 -> x3, starting transfers between devices: none -> 4.71 us  [on_device(): lax.ppermute(pieces[far - 1], 'pix', [(d, (d - 1) % ways) for d in range(...]
    reduce_scatter x1, waiting for transfers between devices: 43.2 us -> 46.1 us  [on_device(): mixed = lax.psum_scatter(terms, 'pix', scatter_dimension=0, tiled=True)]
  transfers between devices with their start and end apart: 4 -> 6, of which waited for: 3 -> 5; matrix products, arithmetic and copies ran while one was open for 3% -> 3% of each run, Pallas kernels for 0% -> 0%
where the time goes in v1:
time: 202 us; the launch traced here: 201 us
  waiting for transfers between devices  80.8 us (40%)
  other arithmetic  57.5 us (28%)
  matrix products  18.1 us (9%)
  local copies, waits for them, and re-layouts  14.8 us (7%)
  between operations  13.5 us (7%)
  starting transfers between devices  10.9 us (5%)
  blocking collectives  5.76 us (3%)
    reduce_sum x1, other arithmetic, on_device(): jnp.sum(values, axis=0)  52.7 us
    reduce_scatter x1, waiting for transfers between devices, on_device(): mixed = lax.psum_scatter(terms, 'pix', scatter_dimension=0, tiled=True)  46.1 us
    ppermute x3, waiting for transfers between devices, on_device(): lax.ppermute(pieces[far - 1], 'pix', [(d, (d - 1) % ways) for d in range(...  18.4 us
    dot_general x1, matrix products, on_device(): terms = jnp.dot(down_weight, hidden, preferred_element_type=jnp.float32)  18.1 us
    ppermute x1, waiting for transfers between devices, with_halo(): lax.ppermute(lax.slice_in_dim(block, block.shape[dim] - width, None, axis...  16.3 us
    unnamed x16, local copies, waits for them, and re-layouts  6.04 us
    psum x1, blocking collectives, on_device(): lax.psum((jnp.sum(values, axis=0), jnp.sum(values * values, axis=0)), 'pix')  5.76 us
    ppermute x1, starting transfers between devices, with_halo(): lax.ppermute(lax.slice_in_dim(block, block.shape[dim] - width, None, axis...  4.9 us
  transfers between devices with their start and end apart: 6, of which 5 were waited for; matrix products, arithmetic and copies ran while one was open for 3% of the time, Pallas kernels for 0%

profile of v1, /device:TPU:0, one launch (start us, length us, event | category | flops | bytes accessed | tf_op | source)
XLA Modules:
  0.0 201.4 jit_solution(1766036209078017531)
XLA Ops:
  6.5 0.0 copy-start.3
  6.5 0.0 reduce-scatter.2.cloned.1.call-start
  6.5 1.7 fusion.113
  8.2 4.9 %collective-permute-start = (bf16[512,3,128]{2,1,0:T(4,128)(2,1)S(1)}, bf16[512,3,128]{2,1,0:T(4,128)(2,1)S(1)}, u32[]{:S(2)}, u32[]{:S(2)}) collective-permute-start(bf16[512,3,128]{2,1,0:T(4,128)(2,1)S(1)} %get-tuple-element.12), channel_id=1, source_target_pairs={{0,1},{1,2},{2,3},{3,4},{4,5},{5,6},{6,7},{8,9},{9,10},{10,11},{11... | collective-permute-start | bytes 1179656 | tf_op jit(solution)/shard_map/ppermute | solution.py:14
  13.1 1.3 collective-permute-start.1
  14.5 1.1 fusion.114
  15.6 0.8 dynamic_slice.10
  16.4 0.8 dynamic_slice.11
  17.1 1.0 fusion.116
  18.1 1.2 fusion.115
  19.2 16.3 %collective-permute-done = bf16[512,3,128]{2,1,0:T(4,128)(2,1)S(1)} collective-permute-done((bf16[512,3,128]{2,1,0:T(4,128)(2,1)S(1)}, bf16[512,3,128]{2,1,0:T(4,128)(2,1)S(1)}, u32[]{:S(2)}, u32[]{:S(2)}) %collective-permute-start) | collective-permute-done | bytes 393248 | tf_op jit(solution)/shard_map/ppermute | solution.py:14
  35.5 0.0 collective-permute-done.1
  35.5 2.2 %maximum_convert_fusion = f32[512,10,128]{2,1,0:T(8,128)S(1)} fusion(bf16[512,3,128]{2,1,0:T(4,128)(2,1)S(1)} %collective-permute-done.1, bf16[512,4,128]{2,1,0:T(4,128)(2,1)} %param.10, bf16[512,3,128]{2,1,0:T(4,128)(2,1)S(1)} %collective-permute-done), kind=kLoop, calls=%fused_computation.52 | loop fusion | flops 3932160 | bytes 3932160 | tf_op jit(solution)/shard_map/convert_element_type | solution.py:37
  37.7 0.0 copy-done.3
  37.7 52.7 %convert_reduce_fusion = (f32[4,128]{1,0:T(4,128)S(1)}, f32[4,128]{1,0:T(4,128)S(1)}, bf16[512,4,128]{2,1,0:T(4,128)(2,1)S(1)}) fusion(f32[512]{0:T(512)S(1)} %copy-done.3, f32[512]{0:T(512)S(1)} %bitcast.107, f32[512]{0:T(512)S(1)} %bitcast.108, f32[512]{0:T(512)S(1)} %bitcast.80, f32[512,10,128]{2,1,0:T(8,128)S(1)} %maximum_convert_fusion, ...), kind=kLoop, calls=%fused_computation.160 | loop fusion | flops 26999808 | bytes 12165120 | tf_op jit(solution)/shard_map/reduce_sum | solution.py:49
  90.4 0.1 convert.2
  90.6 5.8 %all-reduce.1 = (f32[512]{0:T(512)S(1)}, f32[512]{0:T(512)S(1)}) all-reduce(f32[512]{0:T(512)S(1)} %bitcast.129, f32[512]{0:T(512)S(1)} %bitcast.128), channel_id=1, replica_groups=mesh['pix'=4,'chan'=8] {'pix'}, use_global_device_ids=true, to_apply=%region_3.4 | all-reduce | flops 1024 | bytes 8192 | tf_op jit(solution)/shard_map/psum | solution.py:48
  96.3 1.0 constant_dynamic-update-slice_fusion.7
  97.4 0.0 copy-start.4
  97.4 0.9 collective-permute-start.2
  98.3 6.7 %collective-permute-done.2 = bf16[512,512]{1,0:T(8,128)(2,1)S(1)} collective-permute-done((bf16[512,512]{1,0:T(8,128)(2,1)S(1)}, bf16[512,512]{1,0:T(8,128)(2,1)S(1)}, u32[]{:S(2)}, u32[]{:S(2)}) %collective-permute-start.2) | collective-permute-done | bytes 524320 | tf_op jit(solution)/shard_map/ppermute | solution.py:63
  105.0 1.9 collective-permute-start.3
  106.9 6.7 %collective-permute-done.3 = bf16[512,512]{1,0:T(8,128)(2,1)S(1)} collective-permute-done((bf16[512,512]{1,0:T(8,128)(2,1)S(1)}, bf16[512,512]{1,0:T(8,128)(2,1)S(1)}, u32[]{:S(2)}, u32[]{:S(2)}) %collective-permute-start.3) | collective-permute-done | bytes 524320 | tf_op jit(solution)/shard_map/ppermute | solution.py:63
  113.6 1.9 collective-permute-start.4
  115.5 0.8 constant_dynamic-update-slice_fusion.6
  116.3 0.9 constant_dynamic-update-slice_fusion.5
  117.2 5.0 %collective-permute-done.4 = bf16[512,512]{1,0:T(8,128)(2,1)S(1)} collective-permute-done((bf16[512,512]{1,0:T(8,128)(2,1)S(1)}, bf16[512,512]{1,0:T(8,128)(2,1)S(1)}, u32[]{:S(2)}, u32[]{:S(2)}) %collective-permute-start.4) | collective-permute-done | bytes 524320 | tf_op jit(solution)/shard_map/ppermute | solution.py:63
  122.2 0.8 constant_dynamic-update-slice_fusion.4
  123.0 0.9 constant_dynamic-update-slice_fusion.3
  123.9 0.8 constant_dynamic-update-slice_fusion.2
  124.7 0.8 constant_dynamic-update-slice_fusion.1
  125.5 0.9 constant_dynamic-update-slice_fusion
  126.4 0.0 copy-done.4
  126.4 18.1 %convolution_bitcast_fusion = f32[2048,512]{0,1:T(8,128)} fusion(bf16[2048,2048]{1,0:T(8,128)(2,1)} %param.17, bf16[2048,2048]{1,0:T(8,128)(2,1)} %param.15, f32[2048]{0:T(1024)S(1)} %copy-done.4, bf16[4096,512]{1,0:T(8,128)(2,1)} %constant_dynamic-update-slice_fusion, s32[]{:T(128)S(6)} %select_n.19), kind=kOutput, calls=%fused_computation.51 | convolution fusion | flops 8600420352 | bytes 23076868 | tf_op jit(solution)/shard_map/dot_general | solution.py:70
  144.5 0.0 copy-start
  144.5 0.0 copy-start.1
  144.5 0.0 copy-start.2
  144.5 0.0 reduce-scatter.2.cloned.1.call-update
  144.5 1.0 copy-done
  145.5 0.3 copy.11
  145.8 46.1 %reduce-scatter.2.cloned.1.call-done = f32[512,512]{0,1:T(8,128)} async-done(((f32[2048,512]{0,1:T(8,128)}), f32[512,512]{0,1:T(8,128)}) %reduce-scatter.2.cloned.1.call-update) | async-done | bytes 1048592 | tf_op jit(solution)/shard_map/reduce_scatter | solution.py:71
  192.0 0.0 copy-done.1
  192.0 0.0 copy-done.2
  192.0 1.5 fusion.103
  193.5 1.1 copy.12
  (1 shorter events, 0.0 us)
Async XLA Ops:
  6.5 31.2 %copy-start.3 = (f32[512]{0:T(512)S(1)}, f32[512]{0:T(512)}, u32[]{:S(2)}) copy-start(f32[512]{0:T(512)} %param.12) | copy-start | bytes 6148
  6.5 185.4 %reduce-scatter.2.cloned.1.call-start = ((), (), s32[]{:S(2)}) async-start(), calls=%async_computation.1 | async-start | bytes 5242880 | tf_op jit(solution)/shard_map/reduce_scatter | solution.py:71
  8.2 27.3 %collective-permute-start = (bf16[512,3,128]{2,1,0:T(4,128)(2,1)S(1)}, bf16[512,3,128]{2,1,0:T(4,128)(2,1)S(1)}, u32[]{:S(2)}, u32[]{:S(2)}) collective-permute-start(bf16[512,3,128]{2,1,0:T(4,128)(2,1)S(1)} %get-tuple-element.12), channel_id=1, source_target_pairs={{0,1},{1,2},{2,3},{3,4},{4,5},{5,6},{6,7},{8,9},{9,10},{10,11},{11... | collective-permute-start | bytes 1179656 | tf_op jit(solution)/shard_map/ppermute | solution.py:14
  13.1 22.4 %collective-permute-start.1 = (bf16[512,3,128]{2,1,0:T(4,128)(2,1)S(1)}, bf16[512,3,128]{2,1,0:T(4,128)(2,1)S(1)}, u32[]{:S(2)}, u32[]{:S(2)}) collective-permute-start(bf16[512,3,128]{2,1,0:T(4,128)(2,1)S(1)} %get-tuple-element.13), channel_id=1, source_target_pairs={{1,0},{2,1},{3,2},{4,3},{5,4},{6,5},{7,6},{9,8},{10,9},{11,10},{12... | collective-permute-start | bytes 1179656 | tf_op jit(solution)/shard_map/ppermute | solution.py:17
  97.4 29.0 %copy-start.4 = (f32[2048]{0:T(1024)S(1)}, f32[2048]{0:T(1024)}, u32[]{:S(2)}) copy-start(f32[2048]{0:T(1024)} %param.16) | copy-start | bytes 24580
  97.4 7.6 %collective-permute-start.2 = (bf16[512,512]{1,0:T(8,128)(2,1)S(1)}, bf16[512,512]{1,0:T(8,128)(2,1)S(1)}, u32[]{:S(2)}, u32[]{:S(2)}) collective-permute-start(bf16[512,512]{1,0:T(8,128)(2,1)S(1)} %get-tuple-element.10), channel_id=1, source_target_pairs={{0,24},{8,0},{16,8},{24,16},{1,25},{9,1},{17,9},{25,17},{2,26},{10... | collective-permute-start | bytes 1572872 | tf_op jit(solution)/shard_map/ppermute | solution.py:63
  105.0 8.6 %collective-permute-start.3 = (bf16[512,512]{1,0:T(8,128)(2,1)S(1)}, bf16[512,512]{1,0:T(8,128)(2,1)S(1)}, u32[]{:S(2)}, u32[]{:S(2)}) collective-permute-start(bf16[512,512]{1,0:T(8,128)(2,1)S(1)} %collective-permute-done.2), channel_id=1, source_target_pairs={{0,24},{8,0},{16,8},{24,16},{1,25},{9,1},{17,9},{25,17},{2,26},{10... | collective-permute-start | bytes 1572872 | tf_op jit(solution)/shard_map/ppermute | solution.py:63
  113.6 8.6 %collective-permute-start.4 = (bf16[512,512]{1,0:T(8,128)(2,1)S(1)}, bf16[512,512]{1,0:T(8,128)(2,1)S(1)}, u32[]{:S(2)}, u32[]{:S(2)}) collective-permute-start(bf16[512,512]{1,0:T(8,128)(2,1)S(1)} %collective-permute-done.3), channel_id=1, source_target_pairs={{0,24},{8,0},{16,8},{24,16},{1,25},{9,1},{17,9},{25,17},{2,26},{10... | collective-permute-start | bytes 1572872 | tf_op jit(solution)/shard_map/ppermute | solution.py:63
  144.5 1.0 copy-start
  144.5 47.5 %copy-start.1 = (f32[512]{0:T(512)S(1)}, f32[512]{0:T(512)}, u32[]{:S(2)}) copy-start(f32[512]{0:T(512)} %param.18) | copy-start | bytes 6148
  144.5 47.5 %copy-start.2 = (f32[512]{0:T(512)S(1)}, f32[512]{0:T(512)}, u32[]{:S(2)}) copy-start(f32[512]{0:T(512)} %param.19) | copy-start | bytes 6148
Sparse Core Ops, SparseCore 0:
  144.6 47.3 reduce-scatter.1
